TPU v7x, 32 devices: a whole 2x2x4 slice. The times are simulated.
32 devices in a mesh: group: 2 (over y), ctx: 4 (over x, core), tp: 4 (over z).
Axes of the slice: x: 2, y: 2, z: 4, core: 2. Of those that a mesh axis runs over, the one named last changes fastest.
Arguments:
- x_in: bfloat16 [4096, 16384], P(('group', 'ctx'), 'tp'), parts along dimension 0, may hold values from -6 to 6
- bc_in: bfloat16 [4096, 2, 2048], P(('group', 'ctx'), None, 'tp'), parts along dimension 0, may hold values from -6 to 6
- z_in: bfloat16 [4096, 16384], P(('group', 'ctx'), 'tp'), parts along dimension 0, may hold values from -6 to 6
- dt_raw: float32 [4096, 256], P(('group', 'ctx'), 'tp'), parts along dimension 0, may hold values from -3 to 3
- conv_x: bfloat16 [4, 16384], P(None, 'tp'), may hold values from -3 to 3
- conv_bc: bfloat16 [4, 2, 2048], P(None, None, 'tp'), may hold values from -3 to 3
- conv_bias_x: float32 [16384], P('tp'), may hold values from -0.9 to -0.1
- conv_bias_bc: float32 [2, 2048], P(None, 'tp'), may hold values from -0.9 to -0.1
- dt_bias: float32 [256], P('tp'), may hold values from -12 to 2
- a_log: float32 [256], P('tp'), may hold values from -12 to 4
- d_skip: float32 [256], P('tp'), may hold values from 0.5 to 2
- norm_gain: float32 [16384], P('tp'), may hold values from 0.5 to 1.5
Outputs:
- mixed: bfloat16 [4096, 16384], P(('group', 'ctx'), 'tp'), parts along dimension 0
- final_state: float32 [512, 64, 256], P(('group', 'tp'), None, 'ctx'), parts along dimension 0
There are 2 independent parts, one for each index of `group`. A program takes and returns all parts, laid end to end along the dimension named above; an argument that names none is the same for every part. Nothing has to cross between parts.
All inputs are finite; a program needn't handle non-finite values.
Results may differ from a plain program's by a relative error of at most 0.0059.
Values may be sent and summed in bfloat16 or wider, within the bound.
A program may use at most 192 MiB of HBM per device.

v0:
```python
import functools
import math

import jax
import jax.numpy as jnp
from jax import lax
from jax.experimental import pallas as pl
from jax.experimental.pallas import tpu as pltpu
from jax.sharding import PartitionSpec as P

HEAD_DIM = 64
STATE = 256
SPAN = 128
CHUNK = 512
HEADS_CHUNK = CHUNK // HEAD_DIM
HALO = 8
LOG2E = math.log2(math.e)

eps = 1e-05
F32 = jnp.float32
BF16 = jnp.bfloat16


def silu(v):
    half = 0.5 * v
    return half * jnp.tanh(half) + half


def dot(a, b):
    return jnp.dot(a, b, preferred_element_type=F32)


def params():
    return pltpu.CompilerParams(
        dimension_semantics=("arbitrary",), vmem_limit_bytes=48 << 20
    )


def finish_kernel(y_ref, z_ref, c_ref, state_ref, entry_ref, spread_ref, gain_ref, out_ref):
    entry = dot(entry_ref[...], spread_ref[...])
    y = y_ref[...].astype(F32) + entry * dot(c_ref[...], state_ref[...])
    gated = y * silu(z_ref[...].astype(F32))
    meansq = jnp.mean(gated * gated, axis=-1, keepdims=True)
    out_ref[...] = (gated * lax.rsqrt(meansq + eps) * gain_ref[...]).astype(BF16)


def finish(y, z, c_all, state_in, entry, spread, gain):
    rows, channels = y.shape
    groups = c_all.shape[1] // STATE
    width = channels // groups
    heads = entry.shape[1]
    blocks = rows // SPAN
    return pl.pallas_call(
        finish_kernel,
        grid=(groups * blocks,),
        in_specs=[
            pl.BlockSpec((SPAN, width), lambda j: (j % blocks, j // blocks)),
            pl.BlockSpec((SPAN, width), lambda j: (j % blocks, j // blocks)),
            pl.BlockSpec((SPAN, STATE), lambda j: (j % blocks, j // blocks)),
            pl.BlockSpec((STATE, width), lambda j: (0, j // blocks)),
            pl.BlockSpec((SPAN, heads), lambda j: (j % blocks, 0)),
            pl.BlockSpec((heads, width), lambda j: (0, j // blocks)),
            pl.BlockSpec((1, width), lambda j: (0, j // blocks)),
        ],
        out_specs=pl.BlockSpec((SPAN, width), lambda j: (j % blocks, j // blocks)),
        out_shape=jax.ShapeDtypeStruct((rows, channels), BF16),
        compiler_params=params(),
        cost_estimate=pl.CostEstimate(
            flops=2 * rows * channels * STATE, bytes_accessed=6 * rows * channels, transcendentals=rows * channels
        ),
    )(y, z, c_all, state_in, entry, spread, gain)


EDGE = 16
MESH = pl.DeviceIdType.MESH


def conv_rows(read, before, taps, bias, rows, write):
    step = 64
    lag = taps.shape[0] - 1
    for r in range(0, rows, step):
        here = read(r, step).astype(F32)
        window = jnp.concatenate([before, here], axis=0)
        before = here[step - HALO :]
        acc = bias + here * taps[lag][None]
        for k in range(lag):
            at = HALO - lag + k
            acc = acc + window[at : at + step] * taps[k][None]
        write(r, step, silu(acc))


def exact_dot(a, b):
    return jnp.dot(a, b, preferred_element_type=F32, precision=lax.Precision.HIGHEST)


def scan_kernel(
    n,
    x_ref,
    taps_ref,
    bias_ref,
    bc_ref,
    taps_bc_ref,
    bias_bc_ref,
    dt_ref,
    dt_bias_ref,
    a_log_ref,
    skip_ref,
    x_any,
    bc_any,
    y_ref,
    c_out,
    state_out,
    entry_out,
    final_out,
    xc,
    sent,
    came,
    piece,
    st_ref,
    col_ref,
    row_ref,
    tail_dev_ref,
    tail_ref,
    entry_ref,
    fade_ref,
    bt_ref,
    c_ref,
    edge_x,
    edge_bc,
    send_sem,
    recv_sem,
    piece_send,
    piece_recv,
    edge_send,
    edge_recv,
):
    s = pl.program_id(0)
    chunks = sent.shape[0]
    last_step = 2 * chunks - 1
    me = lax.axis_index("ctx")
    rows = x_ref.shape[0]
    spans = rows // SPAN
    heads = dt_ref.shape[1]
    groups = bt_ref.shape[0]
    per = chunks // groups
    share = STATE // n
    right = jnp.minimum(me + 1, n - 1)
    phase = s // chunks
    j = s % chunks

    def edge_copies():
        return [
            pltpu.make_async_remote_copy(
                src_ref=whole.at[pl.ds(rows - EDGE, EDGE)],
                dst_ref=edge,
                send_sem=edge_send.at[i],
                recv_sem=edge_recv.at[i],
                device_id={"ctx": right},
                device_id_type=MESH,
            )
            for i, (whole, edge) in enumerate(((bc_any, edge_bc), (x_any, edge_x)))
        ]

    def onward(c):
        return pltpu.make_async_remote_copy(
            src_ref=sent.at[c],
            dst_ref=came.at[c],
            send_sem=send_sem.at[c],
            recv_sem=recv_sem.at[c],
            device_id={"ctx": right},
            device_id_type=MESH,
        )

    def handed(q, c):
        return pltpu.make_async_remote_copy(
            src_ref=sent.at[c, pl.ds(pl.multiple_of(q * share, share), share)],
            dst_ref=piece.at[c],
            send_sem=piece_send.at[q, c],
            recv_sem=piece_recv.at[c],
            device_id={"ctx": q},
            device_id_type=MESH,
        )

    def spread_of(c):
        shape = (heads, CHUNK)
        return (
            lax.broadcasted_iota(jnp.int32, shape, 1) // HEAD_DIM + c * HEADS_CHUNK
            == lax.broadcasted_iota(jnp.int32, shape, 0)
        ).astype(F32)

    @pl.when(s == 0)
    def _():
        barrier = pltpu.get_barrier_semaphore()
        for k in range(1, n):
            pl.semaphore_signal(
                barrier, inc=1, device_id={"ctx": lax.rem(me + k, n)}, device_id_type=MESH
            )
        pl.semaphore_wait(barrier, n - 1)

        @pl.when(me < n - 1)
        def _():
            for copy in edge_copies():
                copy.start()

        rate = -LOG2E * jnp.exp(a_log_ref[...])
        lower = (
            lax.broadcasted_iota(jnp.int32, (SPAN, SPAN), 0)
            >= lax.broadcasted_iota(jnp.int32, (SPAN, SPAN), 1)
        ).astype(F32)
        steps, sums = [], []
        so_far = jnp.zeros((1, heads), F32)
        starts = []
        for k in range(spans):
            at = slice(k * SPAN, (k + 1) * SPAN)
            v = dt_ref[at] + dt_bias_ref[...]
            step = jnp.maximum(v, 0.0) + jnp.log1p(jnp.exp(-jnp.abs(v)))
            cumul = exact_dot(lower, step * rate)
            last = cumul[SPAN - 1 :]
            tail_ref[at] = (jnp.exp2(last - cumul) * step).astype(BF16)
            entry_ref[at] = jnp.exp2(cumul).astype(BF16)
            entry_out[at] = jnp.exp2(cumul + so_far).astype(BF16)
            fade_ref[k : k + 1] = jnp.exp2(last)
            steps.append(step)
            sums.append(cumul)
            starts.append(so_far)
            so_far = so_far + last
        fade_ref[spans : spans + 1] = jnp.exp2(so_far)
        fade_ref[spans + 1 : spans + 2] = skip_ref[...]
        fade_ref[spans + 2 :] = jnp.zeros((fade_ref.shape[0] - spans - 2, heads), F32)
        for k in range(spans):
            at = slice(k * SPAN, (k + 1) * SPAN)
            tail_dev_ref[at] = (jnp.exp2(so_far - (sums[k] + starts[k])) * steps[k]).astype(BF16)
            for c in range(chunks):
                col_ref[c, at] = sums[k][:, c * HEADS_CHUNK : (c + 1) * HEADS_CHUNK]
            rowed = sums[k] - jnp.log2(steps[k])
            wide = jnp.concatenate([rowed] * (128 // heads), axis=1) if heads < 128 else rowed
            row_ref[:, at] = wide.T[:heads]

        @pl.when(me == 0)
        def _():
            edge_x[...] = jnp.zeros_like(edge_x)
            edge_bc[...] = jnp.zeros_like(edge_bc)
            state_out[...] = jnp.zeros_like(state_out)

        @pl.when(me > 0)
        def _():
            for copy in edge_copies():
                copy.wait_recv()

        for side in range(2):
            for g in range(groups):
                lanes = slice((side * groups + g) * STATE, (side * groups + g + 1) * STATE)

                def write(r, size, value, g=g, side=side):
                    if side == 0:
                        bt_ref[g, :, r : r + size] = value.astype(BF16).astype(F32).T.astype(BF16)
                    else:
                        c_ref[g, r : r + size] = value.astype(BF16)
                        c_out[r : r + size, g * STATE : (g + 1) * STATE] = value.astype(BF16)

                rows_at = SPAN
                lag = taps_bc_ref.shape[0] - 1
                before = edge_bc[:, lanes].astype(F32)[EDGE - HALO :]
                taps = taps_bc_ref[:, lanes].astype(F32)
                for r in range(0, rows, rows_at):
                    here = bc_ref[r : r + rows_at, lanes].astype(F32)
                    window = jnp.concatenate([before, here], axis=0)
                    before = here[rows_at - HALO :]
                    acc = bias_bc_ref[:, lanes] + here * taps[lag][None]
                    for k in range(lag):
                        first = HALO - lag + k
                        acc = acc + window[first : first + rows_at] * taps[k][None]
                    write(r, rows_at, silu(acc))

    def join(c, carry):
        onward(c).wait_recv()
        got = came[c]
        state_out[:, pl.ds(pl.multiple_of(c * CHUNK, CHUNK), CHUNK)] = got
        fades = exact_dot(fade_ref[...], spread_of(c))
        mine = sent[c].astype(F32)
        sent[c] = (fades[spans : spans + 1] * got.astype(F32) + mine).astype(BF16)

        @pl.when(me < n - 1)
        def _():
            onward(c).start()

        @pl.when(me == n - 1)
        def _():
            lax.fori_loop(0, n - 1, lambda q, z: (handed(q, c).start(), z)[1], 0)

        return carry

    base = jnp.where(me == 1, 2, chunks - 3 + me)
    first = jnp.clip(s - base, 0, chunks)
    stop = jnp.where(s == last_step, chunks, jnp.clip(s - base + 1, 0, chunks))
    stop = jnp.where(me == 0, first, stop)
    lax.fori_loop(first, stop, join, 0)

    @pl.when(phase == 0)
    def _():
        spread = spread_of(j).astype(BF16)
        bt = bt_ref.at[j // per]
        taps = taps_ref[...].astype(F32)
        before = edge_x[:, pl.ds(pl.multiple_of(j * CHUNK, CHUNK), CHUNK)].astype(F32)[EDGE - HALO :]

        def write(r, size, value):
            xc[j, r : r + size] = value.astype(BF16)

        conv_rows(lambda r, size: x_ref[r : r + size], before, taps, bias_ref[...], rows, write)
        total = None
        for r in range(0, rows, SPAN):
            weight = dot(tail_dev_ref[r : r + SPAN], spread)
            scaled = (xc[j, r : r + SPAN].astype(F32) * weight).astype(BF16)
            part = dot(bt[:, r : r + SPAN], scaled)
            total = part if total is None else total + part
        sent[j] = total.astype(BF16)

        @pl.when(me == 0)
        def _():
            onward(j).start()

    @pl.when(phase == 1)
    def _():
        spread = spread_of(j)
        fades = exact_dot(fade_ref[...], spread)
        spread = spread.astype(BF16)
        g = j // per
        causal = lax.broadcasted_iota(jnp.int32, (SPAN, SPAN), 0) >= lax.broadcasted_iota(
            jnp.int32, (SPAN, SPAN), 1
        )
        low = lax.broadcasted_iota(jnp.int32, (SPAN, 2 * HEAD_DIM), 1) < HEAD_DIM
        none = jnp.zeros((), BF16)
        head_rows = pl.ds(pl.multiple_of(j * HEADS_CHUNK, HEADS_CHUNK), HEADS_CHUNK)
        for k in range(spans):
            at = slice(k * SPAN, (k + 1) * SPAN)
            c_span = c_ref[g, at]
            b_span = bt_ref[g, :, at]
            scores = dot(c_span, b_span)
            x_span = xc[j, at]
            row_span = row_ref[head_rows, at]
            out = x_span.astype(F32) * fades[spans + 1 : spans + 2]
            if k > 0:
                entry = dot(entry_ref[at], spread)
                out = out + entry * dot(c_span, st_ref[...].astype(BF16))
            for pair in range(HEADS_CHUNK // 2):
                weights = []
                for h in (2 * pair, 2 * pair + 1):
                    spacing = col_ref[j, at, h : h + 1] - row_span[h : h + 1]
                    decay = jnp.exp2(jnp.where(causal, spacing, -jnp.inf))
                    weights.append((decay * scores).astype(BF16))
                lanes = slice(pair * 2 * HEAD_DIM, (pair + 1) * 2 * HEAD_DIM)
                x_pair = x_span[:, lanes]
                stacked = jnp.concatenate(
                    [jnp.where(low, x_pair, none), jnp.where(low, none, x_pair)], axis=0
                )
                within = dot(jnp.concatenate(weights, axis=1), stacked)
                y_ref[at, lanes] = (out[:, lanes] + within).astype(BF16)
            if k < spans - 1:
                weight = dot(tail_ref[at], spread)
                scaled = (x_span.astype(F32) * weight).astype(BF16)
                part = dot(b_span, scaled)
                if k > 0:
                    part = part + fades[k : k + 1] * st_ref[...]
                st_ref[...] = part

    @pl.when(s == last_step)
    def _():
        @pl.when(me < n - 1)
        def _():
            for copy in edge_copies():
                copy.wait_send()
            for c in range(chunks):
                onward(c).wait_send()
            for c in range(chunks):
                handed(0, c).wait_recv()
                final_out[:, c * CHUNK : (c + 1) * CHUNK] = piece[c]

        @pl.when(me == n - 1)
        def _():
            for c in range(chunks):
                lax.fori_loop(0, n - 1, lambda q, z: (handed(q, c).wait_send(), z)[1], 0)
                final_out[:, c * CHUNK : (c + 1) * CHUNK] = sent[c, (n - 1) * share :]


def scan(n, x, taps, bias, bc, taps_bc, bias_bc, dt, dt_bias, a_log, skip):
    rows, channels = x.shape
    chunks = channels // CHUNK
    heads = dt.shape[1]
    width = bc.shape[1]
    groups = width // (2 * STATE)
    share = STATE // n
    spans = rows // SPAN
    turn = lambda s: (0, jnp.minimum(s, chunks - 1))
    still = lambda s: (0, 0)
    return pl.pallas_call(
        functools.partial(scan_kernel, n),
        grid=(2 * chunks,),
        in_specs=[
            pl.BlockSpec((rows, CHUNK), turn),
            pl.BlockSpec((taps.shape[0], CHUNK), turn),
            pl.BlockSpec((1, CHUNK), turn),
            pl.BlockSpec((rows, width), still),
            pl.BlockSpec((taps.shape[0], width), still),
            pl.BlockSpec((1, width), still),
            pl.BlockSpec((rows, heads), still),
            pl.BlockSpec((1, heads), still),
            pl.BlockSpec((1, heads), still),
            pl.BlockSpec((1, heads), still),
            pl.BlockSpec(memory_space=pl.ANY),
            pl.BlockSpec(memory_space=pl.ANY),
        ],
        out_specs=[
            pl.BlockSpec((rows, CHUNK), lambda s: (0, jnp.maximum(s - chunks, 0))),
            pl.BlockSpec((rows, groups * STATE), still),
            pl.BlockSpec((STATE, channels), still),
            pl.BlockSpec((rows, heads), still),
            pl.BlockSpec((share, channels), still),
        ],
        out_shape=[
            jax.ShapeDtypeStruct((rows, channels), BF16),
            jax.ShapeDtypeStruct((rows, groups * STATE), BF16),
            jax.ShapeDtypeStruct((STATE, channels), BF16),
            jax.ShapeDtypeStruct((rows, heads), BF16),
            jax.ShapeDtypeStruct((share, channels), BF16),
        ],
        scratch_shapes=[
            pltpu.VMEM((chunks, rows, CHUNK), BF16),
            pltpu.VMEM((chunks, STATE, CHUNK), BF16),
            pltpu.VMEM((chunks, STATE, CHUNK), BF16),
            pltpu.VMEM((chunks, share, CHUNK), BF16),
            pltpu.VMEM((STATE, CHUNK), F32),
            pltpu.VMEM((chunks, rows, HEADS_CHUNK), F32),
            pltpu.VMEM((heads, rows), F32),
            pltpu.VMEM((rows, heads), BF16),
            pltpu.VMEM((rows, heads), BF16),
            pltpu.VMEM((rows, heads), BF16),
            pltpu.VMEM((-(-(spans + 2) // 8) * 8, heads), F32),
            pltpu.VMEM((groups, STATE, rows), BF16),
            pltpu.VMEM((groups, rows, STATE), BF16),
            pltpu.VMEM((EDGE, channels), BF16),
            pltpu.VMEM((EDGE, width), BF16),
            pltpu.SemaphoreType.DMA((chunks,)),
            pltpu.SemaphoreType.DMA((chunks,)),
            pltpu.SemaphoreType.DMA((n - 1, chunks)),
            pltpu.SemaphoreType.DMA((chunks,)),
            pltpu.SemaphoreType.DMA((2,)),
            pltpu.SemaphoreType.DMA((2,)),
        ],
        compiler_params=pltpu.CompilerParams(
            dimension_semantics=("arbitrary",),
            vmem_limit_bytes=56 << 20,
            collective_id=0,
            has_side_effects=True,
        ),
        cost_estimate=pl.CostEstimate(
            flops=20 * rows * channels * STATE, bytes_accessed=4 * rows * channels, transcendentals=4 * rows * channels
        ),
    )(x, taps, bias, bc, taps_bc, bias_bc, dt, dt_bias, a_log, skip, x, bc)


def per_device(
    x_in,
    bc_in,
    z_in,
    dt_raw,
    conv_x,
    conv_bc,
    conv_bias_x,
    conv_bias_bc,
    dt_bias,
    a_log,
    d_skip,
    norm_gain,
):
    rows, channels = x_in.shape
    heads = dt_raw.shape[1]
    n = lax.axis_size("ctx")
    width = 2 * bc_in.shape[2]
    y, c_all, state_in, entry, final = scan(
        n,
        x_in,
        conv_x,
        conv_bias_x[None],
        bc_in.reshape(rows, width),
        conv_bc.reshape(conv_bc.shape[0], width),
        conv_bias_bc.reshape(1, width),
        dt_raw,
        dt_bias[None],
        a_log[None],
        d_skip[None],
    )
    spread = (
        lax.broadcasted_iota(jnp.int32, (heads, channels), 1) // HEAD_DIM
        == lax.broadcasted_iota(jnp.int32, (heads, channels), 0)
    ).astype(BF16)
    mixed = finish(y, z_in, c_all, state_in, entry, spread, norm_gain[None])
    share = STATE // n
    final_share = final.astype(F32).reshape(share, heads, HEAD_DIM).transpose(1, 2, 0)
    return (mixed, final_share)


def solution(mesh):
    in_specs = (
        P(("group", "ctx"), "tp"),
        P(("group", "ctx"), None, "tp"),
        P(("group", "ctx"), "tp"),
        P(("group", "ctx"), "tp"),
        P(None, "tp"),
        P(None, None, "tp"),
        P("tp"),
        P(None, "tp"),
        P("tp"),
        P("tp"),
        P("tp"),
        P("tp"),
    )
    out_specs = (P(("group", "ctx"), "tp"), P(("group", "tp"), None, "ctx"))
    return jax.shard_map(
        per_device, mesh=mesh, in_specs=in_specs, out_specs=out_specs, check_vma=False
    )
```

profile of v0, /device:TPU:1, one launch (start us, length us, event | category | flops | bytes accessed | tf_op | source)
XLA Modules:
  0.0 68.3 jit_solution(15173419749310287809)
XLA Ops:
  0.6 1.3 %copy.19 = f32[1,1,2,512]{3,1,2,0:T(1,128)} copy(f32[1,1,2,512]{3,2,1,0:T(2,128)} %bitcast.22) | data formatting | bytes 8192
  1.9 1.3 %copy.18 = bf16[1,4,2,512]{3,1,2,0:T(4,128)(2,1)} copy(bf16[1,4,2,512]{3,2,1,0:T(2,128)(2,1)} %bitcast.20) | data formatting | bytes 16384
  3.2 1.7 %copy.14.dt_ref = f32[512,64]{1,0:T(8,128)} copy(f32[512,64]{0,1:T(8,128)} %param.15) | data formatting | bytes 262144 | tf_op args[3]
  5.0 0.1 fusion.spread_ref
  5.1 2.4 %copy.17 = bf16[64,8,2,512]{3,1,2,0:T(8,128)(2,1)} copy(bf16[64,8,2,512]{3,2,1,0:T(2,128)(2,1)} %bitcast.17) | data formatting | bytes 2097152
  7.5 0.0 copy-start.3
  7.5 45.2 %shard_map.131 = (bf16[512,4096]{1,0:T(8,128)(2,1)}, bf16[512,512]{1,0:T(8,128)(2,1)}, bf16[256,4096]{1,0:T(8,128)(2,1)}, bf16[512,64]{1,0:T(8,128)(2,1)}, bf16[64,4096]{1,0:T(8,128)(2,1)}) custom-call(bf16[512,4096]{1,0:T(8,128)(2,1)} %x_any.1, bf16[4,4096]{1,0:T(4,128)(2,1)} %taps_ref.1, f32[1,4096]{1,0:T(1,128)} %bitcast.24, bf16[512,1024]{1,0:T(8,128)(2,1)} %bitcast.18, ...), custom_call_target="tpu_custom_call" | custom-call | flops 10737418240 | bytes 8388608 | tf_op jit(solution)/shard_map/pallas_call | solution.py:395
  52.8 0.0 copy-done.3
  52.8 0.0 copy-start
  52.8 1.6 %copy-done = bf16[256,4096]{1,0:T(8,128)(2,1)S(1)} copy-done((bf16[256,4096]{1,0:T(8,128)(2,1)S(1)}, bf16[256,4096]{1,0:T(8,128)(2,1)}, u32[]{:S(2)}) %copy-start) | copy-done | bytes 2097176
  54.4 0.0 copy-start.1
  54.4 1.0 %copy-done.1 = bf16[512,512]{1,0:T(8,128)(2,1)S(1)} copy-done((bf16[512,512]{1,0:T(8,128)(2,1)S(1)}, bf16[512,512]{1,0:T(8,128)(2,1)}, u32[]{:S(2)}) %copy-start.1) | copy-done | bytes 524312
  55.4 0.0 copy-start.2
  55.4 0.9 %copy-done.2 = bf16[512,64]{1,0:T(8,128)(2,1)S(1)} copy-done((bf16[512,64]{1,0:T(8,128)(2,1)S(1)}, bf16[512,64]{1,0:T(8,128)(2,1)}, u32[]{:S(2)}) %copy-start.2) | copy-done | bytes 65560
  56.3 0.0 copy-start.4
  56.3 10.3 %shard_map.132 = bf16[512,4096]{1,0:T(8,128)(2,1)} custom-call(bf16[512,4096]{1,0:T(8,128)(2,1)} %get-tuple-element.7.y_ref, bf16[512,4096]{1,0:T(8,128)(2,1)} %z_ref.1, bf16[512,512]{1,0:T(8,128)(2,1)S(1)} %copy-done.1, bf16[256,4096]{1,0:T(8,128)(2,1)S(1)} %copy-done, bf16[512,64]{1,0:T(8,128)(2,1)S(1)} %copy-done.2, bf16[64,4096]{1,0:T(8,128)(2,1)S(1)} %fusion.spread_ref, ...), custom_call_target="tpu_custom_call" | custom-call | flops 1073741824 | bytes 12582912 | tf_op jit(solution)/shard_map/pallas_call | solution.py:53
  66.6 0.0 copy-done.4
  66.6 1.7 %copy.16 = f32[64,4096]{0,1:T(8,128)} copy(bf16[64,4096]{1,0:T(8,128)(2,1)S(1)} %copy-done.4) | data formatting | bytes 1572864 | tf_op jit(solution)/shard_map/transpose | solution.py:498
  (2 shorter events, 0.0 us)
Async XLA Ops:
  7.5 45.2 %copy-start.3 = (f32[4096]{0:T(1024)S(1)}, f32[4096]{0:T(1024)}, u32[]{:S(2)}) copy-start(f32[4096]{0:T(1024)} %param.23) | copy-start | bytes 49156
  52.8 1.6 %copy-start = (bf16[256,4096]{1,0:T(8,128)(2,1)S(1)}, bf16[256,4096]{1,0:T(8,128)(2,1)}, u32[]{:S(2)}) copy-start(bf16[256,4096]{1,0:T(8,128)(2,1)} %get-tuple-element.9.state_ref) | copy-start | bytes 6291460
  54.4 1.0 %copy-start.1 = (bf16[512,512]{1,0:T(8,128)(2,1)S(1)}, bf16[512,512]{1,0:T(8,128)(2,1)}, u32[]{:S(2)}) copy-start(bf16[512,512]{1,0:T(8,128)(2,1)} %get-tuple-element.8.c_ref) | copy-start | bytes 1572868
  55.4 0.9 %copy-start.2 = (bf16[512,64]{1,0:T(8,128)(2,1)S(1)}, bf16[512,64]{1,0:T(8,128)(2,1)}, u32[]{:S(2)}) copy-start(bf16[512,64]{1,0:T(8,128)(2,1)} %get-tuple-element.10.entry_ref) | copy-start | bytes 196612
  56.3 10.3 %copy-start.4 = (bf16[64,4096]{1,0:T(8,128)(2,1)S(1)}, bf16[64,4096]{1,0:T(8,128)(2,1)}, u32[]{:S(2)}) copy-start(bf16[64,4096]{1,0:T(8,128)(2,1)} %get-tuple-element.11) | copy-start | bytes 1572868
where the time goes:
time: 68.8 us; the launch traced here: 68.3 us
  Pallas kernels  55.5 us (81%)
  local copies, waits for them, and re-layouts  12 us (17%)
    pallas_call x1, Pallas kernels, scan(): pl.pallas_call(functools.partial(scan_kernel, n), grid=(2 * chunks,), in_...  45.2 us
    unnamed x14, local copies, waits for them, and re-layouts  10.3 us
    pallas_call x1, Pallas kernels, finish(): pl.pallas_call(finish_kernel, grid=(groups * blocks,), in_specs=[pl.Block...  10.3 us
    transpose x1, local copies, waits for them, and re-layouts, per_device(): final.astype(F32).reshape(share, heads, HEAD_DIM).transpose(1, 2, 0)  1.66 us

commit v1 on v0

v1 whole, which is shorter than its diff:
```python
import functools
import math

import jax
import jax.numpy as jnp
from jax import lax
from jax.experimental import pallas as pl
from jax.experimental.pallas import tpu as pltpu
from jax.sharding import PartitionSpec as P

HEAD_DIM = 64
STATE = 256
SPAN = 128
CHUNK = 512
HEADS_CHUNK = CHUNK // HEAD_DIM
HALO = 8
LOG2E = math.log2(math.e)

eps = 1e-05
F32 = jnp.float32
BF16 = jnp.bfloat16


def silu(v):
    half = 0.5 * v
    return half * jnp.tanh(half) + half


def dot(a, b):
    return jnp.dot(a, b, preferred_element_type=F32)


def params():
    return pltpu.CompilerParams(
        dimension_semantics=("arbitrary",), vmem_limit_bytes=48 << 20
    )


def norm_kernel(gated_ref, gain_ref, out_ref):
    gated = gated_ref[...].astype(F32)
    meansq = jnp.mean(gated * gated, axis=-1, keepdims=True)
    out_ref[...] = (gated * lax.rsqrt(meansq + eps) * gain_ref[...]).astype(BF16)


def normed(gated, gain, groups):
    rows, channels = gated.shape
    width = channels // groups
    size = 2 * SPAN
    blocks = rows // size
    block = pl.BlockSpec((size, width), lambda j: (j % blocks, j // blocks))
    return pl.pallas_call(
        norm_kernel,
        grid=(groups * blocks,),
        in_specs=[block, pl.BlockSpec((1, width), lambda j: (0, j // blocks))],
        out_specs=block,
        out_shape=jax.ShapeDtypeStruct((rows, channels), BF16),
        compiler_params=params(),
        cost_estimate=pl.CostEstimate(
            flops=4 * rows * channels, bytes_accessed=4 * rows * channels, transcendentals=rows
        ),
    )(gated, gain)


EDGE = 16
MESH = pl.DeviceIdType.MESH


def conv_rows(read, before, taps, bias, rows, write):
    step = 64
    lag = taps.shape[0] - 1
    for r in range(0, rows, step):
        here = read(r, step).astype(F32)
        window = jnp.concatenate([before, here], axis=0)
        before = here[step - HALO :]
        acc = bias + here * taps[lag][None]
        for k in range(lag):
            at = HALO - lag + k
            acc = acc + window[at : at + step] * taps[k][None]
        write(r, step, silu(acc))


def leading(n, chunks):
    return chunks + max(0, n - 4)


def exact_dot(a, b):
    return jnp.dot(a, b, preferred_element_type=F32, precision=lax.Precision.HIGHEST)


def scan_kernel(
    n,
    x_ref,
    taps_ref,
    bias_ref,
    bc_ref,
    taps_bc_ref,
    bias_bc_ref,
    dt_ref,
    dt_bias_ref,
    a_log_ref,
    skip_ref,
    z_ref,
    x_any,
    bc_any,
    y_ref,
    final_out,
    xc,
    sent,
    came,
    piece,
    local,
    col_ref,
    row_ref,
    tail_ref,
    entry_ref,
    fade_ref,
    bt_ref,
    c_ref,
    edge_x,
    edge_bc,
    send_sem,
    recv_sem,
    piece_send,
    piece_recv,
    edge_send,
    edge_recv,
):
    s = pl.program_id(0)
    chunks = sent.shape[0]
    lead = leading(n, chunks)
    last_step = lead + chunks - 1
    me = lax.axis_index("ctx")
    rows = x_ref.shape[0]
    spans = rows // SPAN
    heads = dt_ref.shape[0]
    groups = bt_ref.shape[0]
    per = chunks // groups
    share = STATE // n
    right = jnp.minimum(me + 1, n - 1)

    def edge_copies():
        return [
            pltpu.make_async_remote_copy(
                src_ref=whole.at[pl.ds(rows - EDGE, EDGE)],
                dst_ref=edge,
                send_sem=edge_send.at[i],
                recv_sem=edge_recv.at[i],
                device_id={"ctx": right},
                device_id_type=MESH,
            )
            for i, (whole, edge) in enumerate(((bc_any, edge_bc), (x_any, edge_x)))
        ]

    def onward(c):
        return pltpu.make_async_remote_copy(
            src_ref=sent.at[c],
            dst_ref=came.at[c],
            send_sem=send_sem.at[c],
            recv_sem=recv_sem.at[c],
            device_id={"ctx": right},
            device_id_type=MESH,
        )

    def handed(q, c):
        return pltpu.make_async_remote_copy(
            src_ref=sent.at[c, pl.ds(pl.multiple_of(q * share, share), share)],
            dst_ref=piece.at[c],
            send_sem=piece_send.at[q, c],
            recv_sem=piece_recv.at[c],
            device_id={"ctx": q},
            device_id_type=MESH,
        )

    def spread_of(c):
        shape = (heads, CHUNK)
        return (
            lax.broadcasted_iota(jnp.int32, shape, 1) // HEAD_DIM + c * HEADS_CHUNK
            == lax.broadcasted_iota(jnp.int32, shape, 0)
        ).astype(F32)

    @pl.when(s == 0)
    def _():
        barrier = pltpu.get_barrier_semaphore()
        for k in range(1, n):
            pl.semaphore_signal(
                barrier, inc=1, device_id={"ctx": lax.rem(me + k, n)}, device_id_type=MESH
            )
        pl.semaphore_wait(barrier, n - 1)

        @pl.when(me < n - 1)
        def _():
            for copy in edge_copies():
                copy.start()

        rate = -LOG2E * jnp.exp(a_log_ref[...])
        lower = (
            lax.broadcasted_iota(jnp.int32, (SPAN, SPAN), 0)
            >= lax.broadcasted_iota(jnp.int32, (SPAN, SPAN), 1)
        ).astype(F32)
        so_far = jnp.zeros((1, heads), F32)
        for k in range(spans):
            at = slice(k * SPAN, (k + 1) * SPAN)
            v = dt_ref[:, at].T + dt_bias_ref[...]
            step = jnp.maximum(v, 0.0) + jnp.log1p(jnp.exp(-jnp.abs(v)))
            cumul = exact_dot(lower, step * rate)
            last = cumul[SPAN - 1 :]
            tail = jnp.exp2(last - cumul) * step
            entry = jnp.exp2(cumul)
            for c in range(chunks):
                mine = slice(c * HEADS_CHUNK, (c + 1) * HEADS_CHUNK)
                col_ref[c, at] = cumul[:, mine]
                tail_ref[c, at] = tail[:, mine]
                entry_ref[c, at] = entry[:, mine]
            rowed = cumul - jnp.log2(step)
            wide = jnp.concatenate([rowed] * (128 // heads), axis=1) if heads < 128 else rowed
            row_ref[:, at] = wide.T[:heads]
            fade_ref[k : k + 1] = jnp.exp2(last)
            fade_ref[spans + 2 + k : spans + 3 + k] = jnp.exp2(so_far)
            so_far = so_far + last
        fade_ref[spans : spans + 1] = jnp.exp2(so_far)
        fade_ref[spans + 1 : spans + 2] = skip_ref[...]
        if fade_ref.shape[0] > 2 * spans + 2:
            fade_ref[2 * spans + 2 :] = jnp.zeros((fade_ref.shape[0] - 2 * spans - 2, heads), F32)

        @pl.when(me == 0)
        def _():
            edge_x[...] = jnp.zeros_like(edge_x)
            edge_bc[...] = jnp.zeros_like(edge_bc)
            came[...] = jnp.zeros_like(came)

        @pl.when(me > 0)
        def _():
            for copy in edge_copies():
                copy.wait_recv()

        for side in range(2):
            for g in range(groups):
                lanes = slice((side * groups + g) * STATE, (side * groups + g + 1) * STATE)
                own = slice(g * STATE, (g + 1) * STATE)

                def write(r, size, value, g=g, side=side):
                    if side == 0:
                        bt_ref[g, :, r : r + size] = value.astype(BF16).astype(F32).T.astype(BF16)
                    else:
                        c_ref[g, r : r + size] = value.astype(BF16)

                rows_at = SPAN
                lag = taps_bc_ref.shape[0] - 1
                before = edge_bc[:, lanes].astype(F32)[EDGE - HALO :]
                taps = taps_bc_ref[:, side, own].astype(F32)
                for r in range(0, rows, rows_at):
                    here = bc_ref[r : r + rows_at, lanes].astype(F32)
                    window = jnp.concatenate([before, here], axis=0)
                    before = here[rows_at - HALO :]
                    acc = bias_bc_ref[side : side + 1, own] + here * taps[lag][None]
                    for k in range(lag):
                        first = HALO - lag + k
                        acc = acc + window[first : first + rows_at] * taps[k][None]
                    write(r, rows_at, silu(acc))

    def join(c, carry):
        onward(c).wait_recv()
        got = came[c]
        fades = exact_dot(fade_ref[...], spread_of(c))
        mine = sent[c].astype(F32)
        sent[c] = (fades[spans : spans + 1] * got.astype(F32) + mine).astype(BF16)

        @pl.when(me < n - 1)
        def _():
            onward(c).start()

        @pl.when(me == n - 1)
        def _():
            lax.fori_loop(0, n - 1, lambda q, z: (handed(q, c).start(), z)[1], 0)

        return carry

    base = jnp.where(me == 1, 2, chunks - 3 + me)
    first = jnp.clip(s - base, 0, chunks)
    stop = jnp.where(s == last_step, chunks, jnp.clip(s - base + 1, 0, chunks))
    stop = jnp.where(me == 0, first, stop)
    lax.fori_loop(first, stop, join, 0)

    low = lax.broadcasted_iota(jnp.int32, (SPAN, 2 * HEAD_DIM), 1) < HEAD_DIM
    pairs = HEADS_CHUNK // 2

    def pair_lanes(pair):
        return slice(pair * 2 * HEAD_DIM, (pair + 1) * 2 * HEAD_DIM)

    def pair_wide(ref, c, at, pair):
        return jnp.where(
            low, ref[c, at, 2 * pair : 2 * pair + 1], ref[c, at, 2 * pair + 1 : 2 * pair + 2]
        )

    @pl.when(s < chunks)
    def _():
        j = s
        bt = bt_ref.at[j // per]
        taps = taps_ref[...].astype(F32)
        before = edge_x[:, pl.ds(pl.multiple_of(j * CHUNK, CHUNK), CHUNK)].astype(F32)[EDGE - HALO :]
        fades = exact_dot(fade_ref[...], spread_of(j))

        def write(r, size, value):
            xc[j, r : r + size] = value.astype(BF16)

        conv_rows(lambda r, size: x_ref[r : r + size], before, taps, bias_ref[...], rows, write)
        state = None
        for k in range(spans):
            at = slice(k * SPAN, (k + 1) * SPAN)
            x_span = xc[j, at].astype(F32)
            scaled = jnp.concatenate(
                [
                    (x_span[:, pair_lanes(pair)] * pair_wide(tail_ref, j, at, pair)).astype(BF16)
                    for pair in range(pairs)
                ],
                axis=1,
            )
            part = dot(bt[:, at], scaled)
            state = part if state is None else fades[k : k + 1] * state + part
            if k < spans - 1:
                local[j, k] = state.astype(BF16)
        sent[j] = state.astype(BF16)

        @pl.when(me == 0)
        def _():
            onward(j).start()

    @pl.when(s >= lead)
    def _():
        j = s - lead
        fades = exact_dot(fade_ref[...], spread_of(j))
        g = j // per
        causal = lax.broadcasted_iota(jnp.int32, (SPAN, SPAN), 0) >= lax.broadcasted_iota(
            jnp.int32, (SPAN, SPAN), 1
        )
        none = jnp.zeros((), BF16)
        head_rows = pl.ds(pl.multiple_of(j * HEADS_CHUNK, HEADS_CHUNK), HEADS_CHUNK)
        for k in range(spans):
            at = slice(k * SPAN, (k + 1) * SPAN)
            c_span = c_ref[g, at]
            scores = dot(c_span, bt_ref[g, :, at])
            row_span = row_ref[head_rows, at]
            if k == 0:
                state = came[j]
            else:
                faded = jnp.broadcast_to(fades[spans + 2 + k : spans + 3 + k], (STATE, CHUNK)).astype(BF16)
                state = local[j, k - 1] + faded * came[j]
            readout = dot(c_span, state)
            for pair in range(pairs):
                lanes = pair_lanes(pair)
                weights = []
                for h in (2 * pair, 2 * pair + 1):
                    spacing = col_ref[j, at, h : h + 1] - row_span[h : h + 1]
                    decay = jnp.exp2(jnp.where(causal, spacing, -jnp.inf))
                    weights.append((decay * scores).astype(BF16))
                x_pair = xc[j, at, lanes]
                stacked = jnp.concatenate(
                    [jnp.where(low, x_pair, none), jnp.where(low, none, x_pair)], axis=0
                )
                within = dot(jnp.concatenate(weights, axis=1), stacked)
                out = (
                    within
                    + x_pair.astype(F32) * fades[spans + 1 : spans + 2, lanes]
                    + pair_wide(entry_ref, j, at, pair) * readout[:, lanes]
                )
                y_ref[at, lanes] = (out * silu(z_ref[at, lanes].astype(F32))).astype(BF16)

    @pl.when(s == last_step)
    def _():
        @pl.when(me < n - 1)
        def _():
            for copy in edge_copies():
                copy.wait_send()
            for c in range(chunks):
                onward(c).wait_send()
            for c in range(chunks):
                handed(0, c).wait_recv()
                final_out[:, c * CHUNK : (c + 1) * CHUNK] = piece[c]

        @pl.when(me == n - 1)
        def _():
            for c in range(chunks):
                lax.fori_loop(0, n - 1, lambda q, z: (handed(q, c).wait_send(), z)[1], 0)
                final_out[:, c * CHUNK : (c + 1) * CHUNK] = sent[c, (n - 1) * share :]


def scan(n, x, taps, bias, bc, taps_bc, bias_bc, dt, dt_bias, a_log, skip, z):
    rows, channels = x.shape
    chunks = channels // CHUNK
    heads = dt.shape[0]
    lead = leading(n, chunks)
    width = bc.shape[1]
    groups = width // (2 * STATE)
    share = STATE // n
    spans = rows // SPAN
    turn = lambda s: (0, jnp.minimum(s, chunks - 1))
    later = lambda s: (0, jnp.maximum(s - lead, 0))
    still = lambda s: (0, 0)
    return pl.pallas_call(
        functools.partial(scan_kernel, n),
        grid=(lead + chunks,),
        in_specs=[
            pl.BlockSpec((rows, CHUNK), turn),
            pl.BlockSpec((taps.shape[0], CHUNK), turn),
            pl.BlockSpec((1, CHUNK), turn),
            pl.BlockSpec((rows, width), still),
            pl.BlockSpec(taps_bc.shape, lambda s: (0, 0, 0)),
            pl.BlockSpec(bias_bc.shape, still),
            pl.BlockSpec((heads, rows), still),
            pl.BlockSpec((1, heads), still),
            pl.BlockSpec((1, heads), still),
            pl.BlockSpec((1, heads), still),
            pl.BlockSpec((rows, CHUNK), later),
            pl.BlockSpec(memory_space=pl.ANY),
            pl.BlockSpec(memory_space=pl.ANY),
        ],
        out_specs=[
            pl.BlockSpec((rows, CHUNK), later),
            pl.BlockSpec((share, channels), still),
        ],
        out_shape=[
            jax.ShapeDtypeStruct((rows, channels), BF16),
            jax.ShapeDtypeStruct((share, channels), BF16),
        ],
        scratch_shapes=[
            pltpu.VMEM((chunks, rows, CHUNK), BF16),
            pltpu.VMEM((chunks, STATE, CHUNK), BF16),
            pltpu.VMEM((chunks, STATE, CHUNK), BF16),
            pltpu.VMEM((chunks, share, CHUNK), BF16),
            pltpu.VMEM((chunks, spans - 1, STATE, CHUNK), BF16),
            pltpu.VMEM((chunks, rows, HEADS_CHUNK), F32),
            pltpu.VMEM((heads, rows), F32),
            pltpu.VMEM((chunks, rows, HEADS_CHUNK), F32),
            pltpu.VMEM((chunks, rows, HEADS_CHUNK), F32),
            pltpu.VMEM((-(-(2 * spans + 2) // 8) * 8, heads), F32),
            pltpu.VMEM((groups, STATE, rows), BF16),
            pltpu.VMEM((groups, rows, STATE), BF16),
            pltpu.VMEM((EDGE, channels), BF16),
            pltpu.VMEM((EDGE, width), BF16),
            pltpu.SemaphoreType.DMA((chunks,)),
            pltpu.SemaphoreType.DMA((chunks,)),
            pltpu.SemaphoreType.DMA((n - 1, chunks)),
            pltpu.SemaphoreType.DMA((chunks,)),
            pltpu.SemaphoreType.DMA((2,)),
            pltpu.SemaphoreType.DMA((2,)),
        ],
        compiler_params=pltpu.CompilerParams(
            dimension_semantics=("arbitrary",),
            vmem_limit_bytes=56 << 20,
            collective_id=0,
            has_side_effects=True,
        ),
        cost_estimate=pl.CostEstimate(
            flops=20 * rows * channels * STATE, bytes_accessed=4 * rows * channels, transcendentals=4 * rows * channels
        ),
    )(x, taps, bias, bc, taps_bc, bias_bc, dt, dt_bias, a_log, skip, z, x, bc)


def per_device(
    x_in,
    bc_in,
    z_in,
    dt_raw,
    conv_x,
    conv_bc,
    conv_bias_x,
    conv_bias_bc,
    dt_bias,
    a_log,
    d_skip,
    norm_gain,
):
    rows, channels = x_in.shape
    heads = dt_raw.shape[1]
    n = lax.axis_size("ctx")
    width = 2 * bc_in.shape[2]
    gated, final = scan(
        n,
        x_in,
        conv_x,
        conv_bias_x[None],
        bc_in.reshape(rows, width),
        conv_bc,
        conv_bias_bc,
        dt_raw.T,
        dt_bias[None],
        a_log[None],
        d_skip[None],
        z_in,
    )
    mixed = normed(gated, norm_gain[None], bc_in.shape[2] // STATE)
    share = STATE // n
    final_share = final.astype(F32).reshape(share, heads, HEAD_DIM).transpose(1, 2, 0)
    return (mixed, final_share)


def solution(mesh):
    in_specs = (
        P(("group", "ctx"), "tp"),
        P(("group", "ctx"), None, "tp"),
        P(("group", "ctx"), "tp"),
        P(("group", "ctx"), "tp"),
        P(None, "tp"),
        P(None, None, "tp"),
        P("tp"),
        P(None, "tp"),
        P("tp"),
        P("tp"),
        P("tp"),
        P("tp"),
    )
    out_specs = (P(("group", "ctx"), "tp"), P(("group", "tp"), None, "ctx"))
    return jax.shard_map(
        per_device, mesh=mesh, in_specs=in_specs, out_specs=out_specs, check_vma=False
    )
```

time: 68.8 us -> 53.1 us (0.77)
  Pallas kernels: 55.5 us -> 45.9 us
  local copies, waits for them, and re-layouts: 12 us -> 6.3 us
    pallas_call x2, Pallas kernels: 55.5 us -> 45.9 us  [the longest x1 42.5 us: scan(): pl.pallas_call(functools.partial(scan_kernel, n), grid=(lead + chunks,),...]
    unnamed x14 -> x7, local copies, waits for them, and re-layouts: 10.3 us -> 4.63 us
where the time goes in v1:
time: 53.1 us; the launch traced here: 52.8 us
  Pallas kernels  45.9 us (86%)
  local copies, waits for them, and re-layouts  6.3 us (12%)
  between operations  0.66 us (1%)
    pallas_call x1, Pallas kernels, scan(): pl.pallas_call(functools.partial(scan_kernel, n), grid=(lead + chunks,),...  42.5 us
    unnamed x7, local copies, waits for them, and re-layouts  4.63 us
    pallas_call x1, Pallas kernels, normed(): pl.pallas_call(norm_kernel, grid=(groups * blocks,), in_specs=[block, pl....  3.42 us
    transpose x1, local copies, waits for them, and re-layouts, per_device(): final.astype(F32).reshape(share, heads, HEAD_DIM).transpose(1, 2, 0)  1.66 us

profile of v1, /device:TPU:1, one launch (start us, length us, event | category | flops | bytes accessed | tf_op | source)
XLA Modules:
  0.0 52.8 jit_solution(15972024234695766869)
XLA Ops:
  0.6 2.4 %copy.16 = bf16[64,8,2,512]{3,1,2,0:T(8,128)(2,1)} copy(bf16[64,8,2,512]{3,2,1,0:T(2,128)(2,1)} %bitcast.13) | data formatting | bytes 2097152
  3.1 0.0 copy-start.1
  3.1 42.5 %shard_map.131 = (bf16[512,4096]{1,0:T(8,128)(2,1)}, bf16[64,4096]{1,0:T(8,128)(2,1)}) custom-call(bf16[512,4096]{1,0:T(8,128)(2,1)} %x_any.1, bf16[4,4096]{1,0:T(4,128)(2,1)} %taps_ref.1, f32[1,4096]{1,0:T(1,128)} %bitcast.17, bf16[512,1024]{1,0:T(8,128)(2,1)} %bitcast.14, bf16[4,2,512]{2,1,0:T(2,128)(2,1)} %taps_bc_ref.1, f32[2,512]{1,0:T(2,128)} %bias_bc_ref.1, ...), custom_call_target="tpu_custom_call" | custom-call | flops 10737418240 | bytes 8388608 | tf_op jit(solution)/shard_map/pallas_call | solution.py:399
  45.6 0.0 copy-done.1
  45.6 0.0 copy-start
  45.6 2.2 %copy-done = bf16[512,4096]{1,0:T(8,128)(2,1)S(1)} copy-done((bf16[512,4096]{1,0:T(8,128)(2,1)S(1)}, bf16[512,4096]{1,0:T(8,128)(2,1)}, u32[]{:S(2)}) %copy-start) | copy-done | bytes 4194328
  47.8 0.0 copy-start.2
  47.8 3.4 %shard_map.132 = bf16[512,4096]{1,0:T(8,128)(2,1)} custom-call(bf16[512,4096]{1,0:T(8,128)(2,1)S(1)} %copy-done, f32[1,4096]{1,0:T(1,128)S(1)} %bitcast.11), custom_call_target="tpu_custom_call" | custom-call | flops 8388608 | bytes 8388608 | tf_op jit(solution)/shard_map/pallas_call | solution.py:51
  51.2 0.0 copy-done.2
  51.2 1.7 %copy.15 = f32[64,4096]{0,1:T(8,128)} copy(bf16[64,4096]{1,0:T(8,128)(2,1)S(1)} %copy-done.2) | data formatting | bytes 1572864 | tf_op jit(solution)/shard_map/transpose | solution.py:493
Async XLA Ops:
  3.1 42.5 %copy-start.1 = (f32[4096]{0:T(1024)S(1)}, f32[4096]{0:T(1024)}, u32[]{:S(2)}) copy-start(f32[4096]{0:T(1024)} %param.23) | copy-start | bytes 49156
  45.6 2.2 %copy-start = (bf16[512,4096]{1,0:T(8,128)(2,1)S(1)}, bf16[512,4096]{1,0:T(8,128)(2,1)}, u32[]{:S(2)}) copy-start(bf16[512,4096]{1,0:T(8,128)(2,1)} %get-tuple-element.4.gated_ref) | copy-start | bytes 12582916
  47.8 3.4 %copy-start.2 = (bf16[64,4096]{1,0:T(8,128)(2,1)S(1)}, bf16[64,4096]{1,0:T(8,128)(2,1)}, u32[]{:S(2)}) copy-start(bf16[64,4096]{1,0:T(8,128)(2,1)} %get-tuple-element.5) | copy-start | bytes 1572868

commit v2 on v1

--- a/solution.py
+++ b/solution.py
@@ -81,6 +81,13 @@
 
 def leading(n, chunks):
     return chunks + max(0, n - 4)
+
+
+def three_terms(a):
+    high = a.astype(BF16)
+    rest = a - high.astype(F32)
+    middle = rest.astype(BF16)
+    return jnp.concatenate([high, middle, (rest - middle.astype(F32)).astype(BF16)], axis=0)
 
 
 def exact_dot(a, b):
@@ -114,6 +121,7 @@
     tail_ref,
     entry_ref,
     fade_ref,
+    fade_terms,
     bt_ref,
     c_ref,
     edge_x,
@@ -176,7 +184,44 @@
         return (
             lax.broadcasted_iota(jnp.int32, shape, 1) // HEAD_DIM + c * HEADS_CHUNK
             == lax.broadcasted_iota(jnp.int32, shape, 0)
+        ).astype(BF16)
+
+    def fades_of(c):
+        terms = dot(fade_terms[...], spread_of(c))
+        size = terms.shape[0] // 3
+        return terms[:size] + terms[size : 2 * size] + terms[2 * size :]
+
+    def span_sums(k):
+        at = slice(k * SPAN, (k + 1) * SPAN)
+        rate = -LOG2E * jnp.exp(a_log_ref[...])
+        lower = (
+            lax.broadcasted_iota(jnp.int32, (SPAN, SPAN), 0)
+            >= lax.broadcasted_iota(jnp.int32, (SPAN, SPAN), 1)
         ).astype(F32)
+        v = dt_ref[:, at].T + dt_bias_ref[...]
+        step = jnp.maximum(v, 0.0) + jnp.log1p(jnp.exp(-jnp.abs(v)))
+        return at, step, exact_dot(lower, step * rate)
+
+    def conv_bc(side):
+        for g in range(groups):
+            lanes = slice((side * groups + g) * STATE, (side * groups + g + 1) * STATE)
+            own = slice(g * STATE, (g + 1) * STATE)
+            lag = taps_bc_ref.shape[0] - 1
+            before = edge_bc[:, lanes].astype(F32)[EDGE - HALO :]
+            taps = taps_bc_ref[:, side, own].astype(F32)
+            for r in range(0, rows, SPAN):
+                here = bc_ref[r : r + SPAN, lanes].astype(F32)
+                window = jnp.concatenate([before, here], axis=0)
+                before = here[SPAN - HALO :]
+                acc = bias_bc_ref[side : side + 1, own] + here * taps[lag][None]
+                for k in range(lag):
+                    first = HALO - lag + k
+                    acc = acc + window[first : first + SPAN] * taps[k][None]
+                value = silu(acc).astype(BF16)
+                if side == 0:
+                    bt_ref[g, :, r : r + SPAN] = value.astype(F32).T.astype(BF16)
+                else:
+                    c_ref[g, r : r + SPAN] = value
 
     @pl.when(s == 0)
     def _():
@@ -192,28 +237,13 @@
             for copy in edge_copies():
                 copy.start()
 
-        rate = -LOG2E * jnp.exp(a_log_ref[...])
-        lower = (
-            lax.broadcasted_iota(jnp.int32, (SPAN, SPAN), 0)
-            >= lax.broadcasted_iota(jnp.int32, (SPAN, SPAN), 1)
-        ).astype(F32)
         so_far = jnp.zeros((1, heads), F32)
         for k in range(spans):
-            at = slice(k * SPAN, (k + 1) * SPAN)
-            v = dt_ref[:, at].T + dt_bias_ref[...]
-            step = jnp.maximum(v, 0.0) + jnp.log1p(jnp.exp(-jnp.abs(v)))
-            cumul = exact_dot(lower, step * rate)
+            at, step, cumul = span_sums(k)
             last = cumul[SPAN - 1 :]
             tail = jnp.exp2(last - cumul) * step
-            entry = jnp.exp2(cumul)
             for c in range(chunks):
-                mine = slice(c * HEADS_CHUNK, (c + 1) * HEADS_CHUNK)
-                col_ref[c, at] = cumul[:, mine]
-                tail_ref[c, at] = tail[:, mine]
-                entry_ref[c, at] = entry[:, mine]
-            rowed = cumul - jnp.log2(step)
-            wide = jnp.concatenate([rowed] * (128 // heads), axis=1) if heads < 128 else rowed
-            row_ref[:, at] = wide.T[:heads]
+                tail_ref[c, at] = tail[:, c * HEADS_CHUNK : (c + 1) * HEADS_CHUNK]
             fade_ref[k : k + 1] = jnp.exp2(last)
             fade_ref[spans + 2 + k : spans + 3 + k] = jnp.exp2(so_far)
             so_far = so_far + last
@@ -222,6 +252,8 @@
         if fade_ref.shape[0] > 2 * spans + 2:
             fade_ref[2 * spans + 2 :] = jnp.zeros((fade_ref.shape[0] - 2 * spans - 2, heads), F32)
 
+        fade_terms[...] = three_terms(fade_ref[...])
+
         @pl.when(me == 0)
         def _():
             edge_x[...] = jnp.zeros_like(edge_x)
@@ -233,35 +265,26 @@
             for copy in edge_copies():
                 copy.wait_recv()
 
-        for side in range(2):
-            for g in range(groups):
-                lanes = slice((side * groups + g) * STATE, (side * groups + g + 1) * STATE)
-                own = slice(g * STATE, (g + 1) * STATE)
-
-                def write(r, size, value, g=g, side=side):
-                    if side == 0:
-                        bt_ref[g, :, r : r + size] = value.astype(BF16).astype(F32).T.astype(BF16)
-                    else:
-                        c_ref[g, r : r + size] = value.astype(BF16)
-
-                rows_at = SPAN
-                lag = taps_bc_ref.shape[0] - 1
-                before = edge_bc[:, lanes].astype(F32)[EDGE - HALO :]
-                taps = taps_bc_ref[:, side, own].astype(F32)
-                for r in range(0, rows, rows_at):
-                    here = bc_ref[r : r + rows_at, lanes].astype(F32)
-                    window = jnp.concatenate([before, here], axis=0)
-                    before = here[rows_at - HALO :]
-                    acc = bias_bc_ref[side : side + 1, own] + here * taps[lag][None]
-                    for k in range(lag):
-                        first = HALO - lag + k
-                        acc = acc + window[first : first + rows_at] * taps[k][None]
-                    write(r, rows_at, silu(acc))
+        conv_bc(0)
+
+    @pl.when(s == 1)
+    def _():
+        for k in range(spans):
+            at, step, cumul = span_sums(k)
+            entry = jnp.exp2(cumul)
+            for c in range(chunks):
+                mine = slice(c * HEADS_CHUNK, (c + 1) * HEADS_CHUNK)
+                col_ref[c, at] = cumul[:, mine]
+                entry_ref[c, at] = entry[:, mine]
+            rowed = cumul - jnp.log2(step)
+            wide = jnp.concatenate([rowed] * (128 // heads), axis=1) if heads < 128 else rowed
+            row_ref[:, at] = wide.T[:heads]
+        conv_bc(1)
 
     def join(c, carry):
         onward(c).wait_recv()
         got = came[c]
-        fades = exact_dot(fade_ref[...], spread_of(c))
+        fades = fades_of(c)
         mine = sent[c].astype(F32)
         sent[c] = (fades[spans : spans + 1] * got.astype(F32) + mine).astype(BF16)
 
@@ -298,7 +321,7 @@
         bt = bt_ref.at[j // per]
         taps = taps_ref[...].astype(F32)
         before = edge_x[:, pl.ds(pl.multiple_of(j * CHUNK, CHUNK), CHUNK)].astype(F32)[EDGE - HALO :]
-        fades = exact_dot(fade_ref[...], spread_of(j))
+        fades = fades_of(j)
 
         def write(r, size, value):
             xc[j, r : r + size] = value.astype(BF16)
@@ -328,7 +351,7 @@
     @pl.when(s >= lead)
     def _():
         j = s - lead
-        fades = exact_dot(fade_ref[...], spread_of(j))
+        fades = fades_of(j)
         g = j // per
         causal = lax.broadcasted_iota(jnp.int32, (SPAN, SPAN), 0) >= lax.broadcasted_iota(
             jnp.int32, (SPAN, SPAN), 1
@@ -432,7 +455,8 @@
             pltpu.VMEM((heads, rows), F32),
             pltpu.VMEM((chunks, rows, HEADS_CHUNK), F32),
             pltpu.VMEM((chunks, rows, HEADS_CHUNK), F32),
-            pltpu.VMEM((-(-(2 * spans + 2) // 8) * 8, heads), F32),
+            pltpu.VMEM((-(-(2 * spans + 2) // 16) * 16, heads), F32),
+            pltpu.VMEM((-(-(2 * spans + 2) // 16) * 48, heads), BF16),
             pltpu.VMEM((groups, STATE, rows), BF16),
             pltpu.VMEM((groups, rows, STATE), BF16),
             pltpu.VMEM((EDGE, channels), BF16),

time: 53.1 us -> 53.8 us (1.013)
  Pallas kernels: 45.9 us -> 46.6 us
    pallas_call x1, Pallas kernels: 42.5 us -> 43.2 us  [scan(): pl.pallas_call(functools.partial(scan_kernel, n), grid=(lead + chunks,),...]
where the time goes in v2:
time: 53.8 us; the launch traced here: 53.5 us
  Pallas kernels  46.6 us (87%)
  local copies, waits for them, and re-layouts  6.3 us (12%)
  between operations  0.66 us (1%)
    pallas_call x1, Pallas kernels, scan(): pl.pallas_call(functools.partial(scan_kernel, n), grid=(lead + chunks,),...  43.2 us
    unnamed x7, local copies, waits for them, and re-layouts  4.63 us
    pallas_call x1, Pallas kernels, normed(): pl.pallas_call(norm_kernel, grid=(groups * blocks,), in_specs=[block, pl....  3.42 us
    transpose x1, local copies, waits for them, and re-layouts, per_device(): final.astype(F32).reshape(share, heads, HEAD_DIM).transpose(1, 2, 0)  1.66 us

profile of v2, /device:TPU:1, one launch (start us, length us, event | category | flops | bytes accessed | tf_op | source)
XLA Modules:
  0.0 53.5 jit_solution(12697829573336780726)
XLA Ops:
  0.6 2.4 %copy.16 = bf16[64,8,2,512]{3,1,2,0:T(8,128)(2,1)} copy(bf16[64,8,2,512]{3,2,1,0:T(2,128)(2,1)} %bitcast.13) | data formatting | bytes 2097152
  3.1 0.0 copy-start.1
  3.1 43.2 %shard_map.131 = (bf16[512,4096]{1,0:T(8,128)(2,1)}, bf16[64,4096]{1,0:T(8,128)(2,1)}) custom-call(bf16[512,4096]{1,0:T(8,128)(2,1)} %x_any.1, bf16[4,4096]{1,0:T(4,128)(2,1)} %taps_ref.1, f32[1,4096]{1,0:T(1,128)} %bitcast.17, bf16[512,1024]{1,0:T(8,128)(2,1)} %bitcast.14, bf16[4,2,512]{2,1,0:T(2,128)(2,1)} %taps_bc_ref.1, f32[2,512]{1,0:T(2,128)} %bias_bc_ref.1, ...), custom_call_target="tpu_custom_call" | custom-call | flops 10737418240 | bytes 8388608 | tf_op jit(solution)/shard_map/pallas_call | solution.py:422
  46.2 0.0 copy-done.1
  46.3 0.0 copy-start
  46.3 2.2 %copy-done = bf16[512,4096]{1,0:T(8,128)(2,1)S(1)} copy-done((bf16[512,4096]{1,0:T(8,128)(2,1)S(1)}, bf16[512,4096]{1,0:T(8,128)(2,1)}, u32[]{:S(2)}) %copy-start) | copy-done | bytes 4194328
  48.4 0.0 copy-start.2
  48.5 3.4 %shard_map.132 = bf16[512,4096]{1,0:T(8,128)(2,1)} custom-call(bf16[512,4096]{1,0:T(8,128)(2,1)S(1)} %copy-done, f32[1,4096]{1,0:T(1,128)S(1)} %bitcast.11), custom_call_target="tpu_custom_call" | custom-call | flops 8388608 | bytes 8388608 | tf_op jit(solution)/shard_map/pallas_call | solution.py:51
  51.9 0.0 copy-done.2
  51.9 1.7 %copy.15 = f32[64,4096]{0,1:T(8,128)} copy(bf16[64,4096]{1,0:T(8,128)(2,1)S(1)} %copy-done.2) | data formatting | bytes 1572864 | tf_op jit(solution)/shard_map/transpose | solution.py:517
Async XLA Ops:
  3.1 43.2 %copy-start.1 = (f32[4096]{0:T(1024)S(1)}, f32[4096]{0:T(1024)}, u32[]{:S(2)}) copy-start(f32[4096]{0:T(1024)} %param.23) | copy-start | bytes 49156
  46.3 2.2 %copy-start = (bf16[512,4096]{1,0:T(8,128)(2,1)S(1)}, bf16[512,4096]{1,0:T(8,128)(2,1)}, u32[]{:S(2)}) copy-start(bf16[512,4096]{1,0:T(8,128)(2,1)} %get-tuple-element.4.gated_ref) | copy-start | bytes 12582916
  48.4 3.4 %copy-start.2 = (bf16[64,4096]{1,0:T(8,128)(2,1)S(1)}, bf16[64,4096]{1,0:T(8,128)(2,1)}, u32[]{:S(2)}) copy-start(bf16[64,4096]{1,0:T(8,128)(2,1)} %get-tuple-element.5) | copy-start | bytes 1572868
